TPU v7x, 32 devices: a whole 2x2x4 slice. The times are simulated.
32 devices in a mesh: freq: 2 (over x), tile: 16 (over z, y, core).
Axes of the slice: x: 2, y: 2, z: 4, core: 2. Of those that a mesh axis runs over, the one named last changes fastest.
Arguments:
- data: float32 [4, 2048, 256], P('freq', 'tile'), parts along dimension 0, may hold values from -6 to 6
- x_init: float32 [4, 8192, 256], P('freq', 'tile'), parts along dimension 0, may hold values from -6 to 6
- ufac: bfloat16 [4, 2048, 256], P('freq', 'tile'), parts along dimension 0, may hold values from -0.1875 to 0.1875
- vfac: bfloat16 [4, 4, 16, 8192], P('freq', None, None, 'tile'), parts along dimension 0, may hold values from -0.25 to 0.25
Outputs:
- solution: float32 [4, 8192, 256], P('freq', 'tile'), parts along dimension 0
- residual: float32 [4, 2048, 256], P('freq', 'tile'), parts along dimension 0
There are 2 independent parts, one for each index of `freq`. A program takes and returns all parts, laid end to end along the dimension named above; each array names one. Nothing has to cross between parts.
All inputs are finite; a program needn't handle non-finite values.
Results may differ from a plain program's by a relative error of at most 0.0058.
Values may be sent and summed in bfloat16 or wider, within the bound.
No kernel may reach another device: no remote copies, remote signals or barrier semaphores. Data moves between devices by JAX's collectives and lax.ppermute only.
A program may use at most 64 MiB of HBM per device.

v0:
```python
import jax
import jax.numpy as jnp
from jax import lax
from jax.sharding import PartitionSpec as P

QV = 4
ITERS = 2


step_size = 0.4
threshold = 0.4


def complex_product(pattern, factors, vectors, conjugate):

    def single(factor_part, vector_part):
        return jnp.einsum(pattern, factor_part, vector_part, preferred_element_type=jnp.float32)

    if conjugate:
        real_part = single(factors[0], vectors[0]) + single(factors[1], vectors[1])
        imag_part = single(factors[0], vectors[1]) - single(factors[1], vectors[0])
    else:
        real_part = single(factors[0], vectors[0]) - single(factors[1], vectors[1])
        imag_part = single(factors[0], vectors[1]) + single(factors[1], vectors[0])
    return jnp.stack([real_part, imag_part])


def shrink(values):
    magnitude = jnp.sqrt(values[0] * values[0] + values[1] * values[1])
    shrink_factor = jnp.maximum(magnitude - threshold, 0.0) / jnp.maximum(magnitude, threshold)
    return values * shrink_factor


def body(data, x_init, ufac, vfac):
    tile_count = lax.axis_size("tile")
    tile_rows = vfac.shape[1]
    rank_width = vfac.shape[2]
    point_count = x_init.shape[2]
    estimate = x_init
    misfit = data
    for iteration in range(ITERS):
        xlow = estimate.astype(jnp.bfloat16)
        coeffs = complex_product("irk,kv->irv", vfac, xlow, True).astype(jnp.bfloat16)
        repeated = jnp.repeat(coeffs, QV, axis=1)
        received = lax.all_to_all(repeated, "tile", split_axis=1, concat_axis=1, tiled=True)
        flat_coeffs = received.reshape(2, tile_count * rank_width, point_count)
        predicted = complex_product("tk,kv->tv", ufac, flat_coeffs, False)
        misfit = data - predicted
        misfit_low = misfit.astype(jnp.bfloat16)
        partial_value = complex_product("tk,tv->kv", ufac, misfit_low, True).reshape(
            2, tile_count, rank_width, point_count
        )
        gathered = lax.all_to_all(partial_value, "tile", split_axis=1, concat_axis=1, tiled=True)
        summed = (
            gathered.reshape(2, tile_rows, QV, rank_width, point_count)
            .sum(axis=2)
            .astype(jnp.bfloat16)
        )
        gradient = complex_product("irk,irv->kv", vfac, summed, False)
        estimate = shrink(estimate + step_size * gradient)
    return (estimate, misfit)


def solution(mesh):
    in_specs = (
        P("freq", "tile", None),
        P("freq", "tile", None),
        P("freq", "tile", None),
        P("freq", None, None, "tile"),
    )
    out_specs = (P("freq", "tile", None), P("freq", "tile", None))
    return jax.shard_map(body, mesh=mesh, in_specs=in_specs, out_specs=out_specs, check_vma=False)
```

profile of v0, /device:TPU:0, one launch (start us, length us, event | category | flops | bytes accessed | tf_op | source)
XLA Modules:
  0.0 85.4 jit_solution(18116899990691036280)
XLA Ops:
  0.6 1.3 %convert_element_type.20 = bf16[2,512,256]{2,1,0:T(8,128)(2,1)S(1)} convert(f32[2,512,256]{2,1,0:T(8,128)} %param.5) | non-fusion elementwise | flops 262144 | bytes 1572864 | tf_op jit(solution)/shard_map/convert_element_type | solution.py:42
  2.7 0.7 broadcast_in_dim.8
  3.4 7.5 %all-to-all-start = ((bf16[2,16,16,256]{3,2,0,1:T(8,128)(2,1)}), bf16[2,16,16,256]{3,2,0,1:T(8,128)(2,1)S(1)}, u32[]{:S(2)}, u32[]{:S(2)}) async-start(bf16[2,16,16,256]{3,2,0,1:T(8,128)(2,1)} %bitcast.8), calls=%async_computation | async-start | bytes 524288 | tf_op jit(solution)/shard_map/all_to_all | solution.py:45
  11.1 9.9 %all-to-all-done = bf16[2,16,16,256]{3,2,0,1:T(8,128)(2,1)S(1)} async-done(((bf16[2,16,16,256]{3,2,0,1:T(8,128)(2,1)}), bf16[2,16,16,256]{3,2,0,1:T(8,128)(2,1)S(1)}, u32[]{:S(2)}, u32[]{:S(2)}) %all-to-all-start) | async-done | bytes 262176 | tf_op jit(solution)/shard_map/all_to_all | solution.py:45
  22.4 0.2 convolution_subtract_fusion.1
  22.7 0.2 convolution_add_fusion.1
  22.9 0.8 pad_maximum_fusion
  23.8 3.6 %all-to-all-start.1 = ((f32[2,16,16,256]{3,2,0,1:T(8,128)}), f32[2,16,16,256]{3,2,0,1:T(8,128)S(1)}, u32[]{:S(2)}, u32[]{:S(2)}) async-start(f32[2,16,16,256]{3,2,0,1:T(8,128)} %pad_maximum_fusion), calls=%async_computation.1 | async-start | bytes 1048576 | tf_op jit(solution)/shard_map/all_to_all | solution.py:53
  27.3 0.3 copy.35
  27.7 13.9 %all-to-all-done.1 = f32[2,16,16,256]{3,2,0,1:T(8,128)S(1)} async-done(((f32[2,16,16,256]{3,2,0,1:T(8,128)}), f32[2,16,16,256]{3,2,0,1:T(8,128)S(1)}, u32[]{:S(2)}, u32[]{:S(2)}) %all-to-all-start.1) | async-done | bytes 524320 | tf_op jit(solution)/shard_map/all_to_all | solution.py:53
  41.6 0.2 convolution_bitcast_fusion.6
  41.9 0.2 convolution_bitcast_fusion.4
  42.1 0.3 fusion.1
  42.4 0.2 fusion.3
  42.9 0.3 divide_bitcast_fusion.1
  43.1 0.3 multiply_convert_fusion
  44.3 13.9 %all_to_all.20 = bf16[2,16,16,256]{3,2,0,1:T(8,128)(2,1)S(1)} all-to-all(bf16[2,16,16,256]{3,2,0,1:T(8,128)(2,1)S(1)} %bitcast.250), channel_id=1, replica_groups=mesh['freq'=2,'tile'=16] {'tile'}, dimensions={1} | all-to-all | bytes 524288 | tf_op jit(solution)/shard_map/all_to_all | solution.py:45
  59.2 0.7 fusion.103
  60.4 0.2 convolution_subtract_fusion
  60.6 0.2 convolution_add_fusion
  60.8 0.8 pad_maximum_fusion.1
  61.7 3.7 %all-to-all-start.3 = ((f32[2,16,16,256]{3,2,0,1:T(8,128)}), f32[2,16,16,256]{3,2,0,1:T(8,128)S(1)}, u32[]{:S(2)}, u32[]{:S(2)}) async-start(f32[2,16,16,256]{3,2,0,1:T(8,128)} %pad_maximum_fusion.1), calls=%async_computation.3 | async-start | bytes 1048576 | tf_op jit(solution)/shard_map/all_to_all | solution.py:53
  65.4 0.8 copy.46
  66.2 13.4 %all-to-all-done.3 = f32[2,16,16,256]{3,2,0,1:T(8,128)S(1)} async-done(((f32[2,16,16,256]{3,2,0,1:T(8,128)}), f32[2,16,16,256]{3,2,0,1:T(8,128)S(1)}, u32[]{:S(2)}, u32[]{:S(2)}) %all-to-all-start.3) | async-done | bytes 524320 | tf_op jit(solution)/shard_map/all_to_all | solution.py:53
  79.7 0.2 convolution_bitcast_fusion.2
  79.9 0.2 convolution_bitcast_fusion
  80.2 0.3 fusion.5
  80.4 0.2 fusion.7
  80.7 0.4 fusion.21
  81.1 0.3 divide_bitcast_fusion
  81.4 1.5 %broadcast_multiply_fusion = f32[2,512,256]{1,2,0:T(8,128)} fusion(f32[512,256]{0,1:T(8,128)S(1)} %divide_bitcast_fusion, f32[1,512,256]{1,2,0:T(8,128)S(1)} %fusion.7, f32[1,512,256]{1,2,0:T(8,128)S(1)} %fusion.5, f32[512,256]{0,1:T(8,128)S(1)} %divide_bitcast_fusion.1, f32[2,512,256]{1,2,0:T(8,128)S(1)} %copy.35, f32[1,512,256]{1,2,0:T(8,128)S(1)} %fusion.3, ...), kind=kLoop, calls=%fused_computation.57 | loop fusion | flops 2097152 | bytes 5242880 | tf_op jit(solution)/shard_map/mul | solution.py:31
  82.9 2.5 %copy.45 = f32[2,512,256]{2,1,0:T(8,128)} copy(f32[2,512,256]{1,2,0:T(8,128)} %broadcast_multiply_fusion) | data formatting | bytes 2097152
  (44 shorter events, 4.7 us)
Async XLA Ops:
  0.6 1.3 %copy-start.2 = (bf16[2,4,16,512]{3,2,1,0:T(8,128)(2,1)S(1)}, bf16[2,4,16,512]{3,2,1,0:T(8,128)(2,1)}, u32[]{:S(2)}) copy-start(bf16[2,4,16,512]{3,2,1,0:T(8,128)(2,1)} %param.7) | copy-start | bytes 393220
  3.4 7.6 %copy-start.5 = (f32[2,128,256]{2,1,0:T(8,128)S(1)}, f32[2,128,256]{2,1,0:T(8,128)}, u32[]{:S(2)}) copy-start(f32[2,128,256]{2,1,0:T(8,128)} %param.4) | copy-start | bytes 786436
  3.4 17.6 %all-to-all-start = ((bf16[2,16,16,256]{3,2,0,1:T(8,128)(2,1)}), bf16[2,16,16,256]{3,2,0,1:T(8,128)(2,1)S(1)}, u32[]{:S(2)}, u32[]{:S(2)}) async-start(bf16[2,16,16,256]{3,2,0,1:T(8,128)(2,1)} %bitcast.8), calls=%async_computation | async-start | bytes 524288 | tf_op jit(solution)/shard_map/all_to_all | solution.py:45
  11.1 9.9 %copy-start = (bf16[2,128,256]{2,1,0:T(8,128)(2,1)S(1)}, bf16[2,128,256]{2,1,0:T(8,128)(2,1)}, u32[]{:S(2)}) copy-start(bf16[2,128,256]{2,1,0:T(8,128)(2,1)} %param.6) | copy-start | bytes 393220
  22.9 4.4 %copy-start.1 = (f32[2,512,256]{2,1,0:T(8,128)S(1)}, f32[2,512,256]{2,1,0:T(8,128)}, u32[]{:S(2)}) copy-start(f32[2,512,256]{2,1,0:T(8,128)} %param.5) | copy-start | bytes 3145732
  23.8 17.8 %all-to-all-start.1 = ((f32[2,16,16,256]{3,2,0,1:T(8,128)}), f32[2,16,16,256]{3,2,0,1:T(8,128)S(1)}, u32[]{:S(2)}, u32[]{:S(2)}) async-start(f32[2,16,16,256]{3,2,0,1:T(8,128)} %pad_maximum_fusion), calls=%async_computation.1 | async-start | bytes 1048576 | tf_op jit(solution)/shard_map/all_to_all | solution.py:53
  61.7 3.7 %copy-start.4 = (f32[2,128,256]{1,2,0:T(8,128)S(1)}, f32[2,128,256]{1,2,0:T(8,128)}, u32[]{:S(2)}) copy-start(f32[2,128,256]{1,2,0:T(8,128)} %get-tuple-element.9) | copy-start | bytes 786436
  61.7 17.9 %all-to-all-start.3 = ((f32[2,16,16,256]{3,2,0,1:T(8,128)}), f32[2,16,16,256]{3,2,0,1:T(8,128)S(1)}, u32[]{:S(2)}, u32[]{:S(2)}) async-start(f32[2,16,16,256]{3,2,0,1:T(8,128)} %pad_maximum_fusion.1), calls=%async_computation.3 | async-start | bytes 1048576 | tf_op jit(solution)/shard_map/all_to_all | solution.py:53
  66.2 13.4 %copy-start.3 = (bf16[2,4,16,512]{3,2,1,0:T(8,128)(2,1)S(1)}, bf16[2,4,16,512]{3,2,1,0:T(8,128)(2,1)}, u32[]{:S(2)}) copy-start(bf16[2,4,16,512]{3,2,1,0:T(8,128)(2,1)} %param.7) | copy-start | bytes 393220
where the time goes:
time: 85.9 us; the launch traced here: 85.4 us
  waiting for transfers between devices  37.1 us (43%)
  starting transfers between devices  14.8 us (17%)
  blocking collectives  13.9 us (16%)
  matrix products  7.03 us (8%)
  other arithmetic  6.81 us (8%)
  local copies, waits for them, and re-layouts  4.65 us (5%)
  between operations  1.04 us (1%)
    all_to_all x2, waiting for transfers between devices, body(): lax.all_to_all(partial_value, 'tile', split_axis=1, concat_axis=1, tiled=...  27.3 us
    all_to_all x1, blocking collectives, body(): lax.all_to_all(repeated, 'tile', split_axis=1, concat_axis=1, tiled=True)  13.9 us
    all_to_all x1, waiting for transfers between devices, body(): lax.all_to_all(repeated, 'tile', split_axis=1, concat_axis=1, tiled=True)  9.86 us
    all_to_all x1, starting transfers between devices, body(): lax.all_to_all(repeated, 'tile', split_axis=1, concat_axis=1, tiled=True)  7.55 us
    all_to_all x2, starting transfers between devices, body(): lax.all_to_all(partial_value, 'tile', split_axis=1, concat_axis=1, tiled=...  7.28 us
    dot_general x32, matrix products, single(): jnp.einsum(pattern, factor_part, vector_part, preferred_element_type=jnp....  7.03 us
    unnamed x16, local copies, waits for them, and re-layouts  3.85 us
    mul x3, other arithmetic, shrink(): return values * shrink_factor  1.99 us
  transfers between devices with their start and end apart: 3, of which 3 were waited for; matrix products, arithmetic and copies ran while one was open for 2% of the time, Pallas kernels for 0%

commit v1 on v0

v1 whole, which is shorter than its diff:
```python
import functools

import jax
import jax.numpy as jnp
from jax import lax
from jax.experimental import pallas as pl
from jax.experimental.pallas import tpu as pltpu
from jax.sharding import PartitionSpec as P

ITERS = 2
STEP = 0.4
THRESHOLD = 0.4

f32 = jnp.float32
bf16 = jnp.bfloat16


def dot(a, b, dims=((1,), (0,))):
    return lax.dot_general(a, b, (dims, ((), ())), preferred_element_type=f32)


def swap_halves(a):
    return pltpu.roll(a, a.shape[1] // 2, 1)


def left_half(a):
    return lax.broadcasted_iota(jnp.int32, a.shape, 1) < a.shape[1] // 2


def times_i(a):
    s = swap_halves(a)
    return jnp.where(left_half(a), -s, s)


def interleave(re, im):
    low = left_half(re)
    return (
        jnp.where(low, re, swap_halves(im)),
        jnp.where(low, swap_halves(re), im),
    )


def slices_of(re, im, width):
    out = []
    for k in range(re.shape[1] // (2 * width)):
        cut = slice(2 * width * k, 2 * width * (k + 1))
        out.extend(interleave(re[:, cut], im[:, cut]))
    return out


def group_index(group):
    return lax.rem(lax.axis_index("tile"), group)


def prepare_kernel(data, ufac, to_far, to_near, own, *, group, width):
    rows = data.shape[1]
    folds = ufac.shape[2] // (4 * width)
    step = rows // folds
    q = group_index(group)
    stage = slices_of(data[0], data[1], width)

    def place(scratch):
        for s, block in enumerate(stage):
            scratch[jnp.bitwise_xor(q, s)] = block
        own[...] = scratch[0]

        def split(block):
            high = block.astype(bf16)
            low = (block - high.astype(f32)).astype(bf16)
            return high, low

        for ref, base, b in ((to_near, 0, 1), (to_far, 0, 2), (to_far, step, 3)):
            high, low = split(scratch[b])
            for g in range(folds):
                cut = slice(g * step, (g + 1) * step)
                lane = 4 * width * g
                ref[base:base + step, lane:lane + 2 * width] = high[cut]
                ref[base:base + step, lane + 2 * width:lane + 4 * width] = low[cut]

    pl.run_scoped(place, pltpu.VMEM((group, rows, 2 * width), f32))
    for part in range(2):
        to_near[step + rows * part:step + rows * (part + 1)] = ufac[part]
        to_far[2 * step + rows * part:2 * step + rows * (part + 1)] = ufac[part]


def send_coeffs(vcat, xr, xi, out, *, group, width):
    half = vcat.shape[0] // 2
    t1 = dot(vcat, xr)
    t2 = dot(vcat, xi)
    cr = t1[:half] + t2[half:]
    ci = t2[:half] - t1[half:]
    rank = out.shape[1]
    blocks = slices_of(cr, ci, width)
    for i in range(half // rank):
        for q in range(group):
            out[i * group + q] = blocks[q][i * rank:(i + 1) * rank].astype(bf16)


def flat_factors(vfac):
    parts, rows, rank, count = vfac.shape
    return vfac[...].reshape(parts * rows * rank, count)


def first_kernel(x, vfac, out, *, group, width):
    send_coeffs(flat_factors(vfac), x[0].astype(bf16), x[1].astype(bf16), out, group=group, width=width)


def row_kernel(coeffs, own, ufac, near, far, far_near, adjoint, *maybe_misfit, width):
    lanes = 2 * width
    rows = own.shape[0]
    c = coeffs[...].reshape(-1, lanes)
    ci = times_i(c.astype(f32)).astype(bf16)

    folds = ufac.shape[2] // (2 * lanes)
    step = rows // folds

    def joined(ref, base):
        cuts = [ref[base:base + step, 2 * lanes * g:2 * lanes * (g + 1)].astype(f32) for g in range(folds)]
        pair = jnp.concatenate(cuts, axis=0)
        return pair[:, :lanes] + pair[:, lanes:]

    def factors(ref, base):
        return ref[base:base + rows], ref[base + rows:base + 2 * rows]

    blocks = (
        (own[...], (ufac[0], ufac[1])),
        (joined(near, 0), factors(near, step)),
        (joined(far, 0), factors(far, 2 * step)),
        (joined(far_near, step), factors(far_near, 2 * step)),
    )
    total = None
    for b, (wave, (ur, ui)) in enumerate(blocks):
        misfit = wave - (dot(ur, c) + dot(ui, ci))
        if maybe_misfit:
            maybe_misfit[0][b] = misfit
        mt = misfit.T.astype(bf16)
        mr, mi = mt[:width], mt[width:]
        turned = jnp.concatenate([mi, -mr], axis=0)
        term = dot(mt, ur) + dot(turned, ui)
        total = term if total is None else total + term
    flat = total.T.astype(bf16)
    rank = adjoint.shape[1]
    for j in range(adjoint.shape[0]):
        adjoint[j] = flat[j * rank:(j + 1) * rank]


def updated(adjoint, x, vcat, *, group, width):
    count, rank, lanes = adjoint.shape
    rows = count // group
    a = adjoint[...].astype(f32).reshape(rows, group, rank, lanes)
    re, im = [], []
    for k in range(group // 2):
        even = a[:, 2 * k].reshape(rows * rank, lanes)
        odd = a[:, 2 * k + 1].reshape(rows * rank, lanes)
        r, i = interleave(even, odd)
        re.append(r)
        im.append(i)
    re = jnp.concatenate(re, axis=1)
    im = jnp.concatenate(im, axis=1)
    real_side = jnp.concatenate([re, -im], axis=0).astype(bf16)
    imag_side = jnp.concatenate([im, re], axis=0).astype(bf16)
    gr = dot(vcat, real_side, ((0,), (0,)))
    gi = dot(vcat, imag_side, ((0,), (0,)))
    sr = x[0] + STEP * gr
    si = x[1] + STEP * gi
    magnitude = jnp.sqrt(sr * sr + si * si)
    factor = jnp.maximum(magnitude - THRESHOLD, 0.0) / jnp.maximum(magnitude, THRESHOLD)
    return sr * factor, si * factor


def middle_kernel(adjoint, x, vfac, x_new, out, *, group, width):
    vcat = flat_factors(vfac)
    xr, xi = updated(adjoint, x, vcat, group=group, width=width)
    x_new[0] = xr
    x_new[1] = xi
    send_coeffs(vcat, xr.astype(bf16), xi.astype(bf16), out, group=group, width=width)


def last_kernel(adjoint, x, vfac, x_new, *, group, width):
    xr, xi = updated(adjoint, x, flat_factors(vfac), group=group, width=width)
    x_new[0] = xr
    x_new[1] = xi


def residual_kernel(misfit, near, far, far_near, out, *, group, width):
    q = group_index(group)

    def place(scratch):
        scratch[0] = misfit[0]
        scratch[1] = near[...]
        scratch[2] = far[0]
        scratch[3] = far_near[1]
        pieces = [scratch[jnp.bitwise_xor(q, s)] for s in range(group)]
        for k in range(group // 2):
            re, im = interleave(pieces[2 * k], pieces[2 * k + 1])
            out[0, :, 2 * width * k:2 * width * (k + 1)] = re
            out[1, :, 2 * width * k:2 * width * (k + 1)] = im

    pl.run_scoped(place, pltpu.VMEM(misfit.shape, f32))


def call(kernel, out_shape, *args, **static):
    return pl.pallas_call(
        functools.partial(kernel, **static),
        out_shape=out_shape,
        name=kernel.__name__,
    )(*args)


def body(data, x_init, ufac, vfac):
    tiles = lax.axis_size("tile")
    tile_rows, rank, _ = vfac.shape[1:]
    rows = data.shape[1]
    points = data.shape[2]
    group = tiles // tile_rows
    assert group == 4
    width = points // group
    lanes = 2 * width
    static = dict(group=group, width=width)
    shape = jax.ShapeDtypeStruct

    def exchange(value, bit):
        return lax.ppermute(value, "tile", [(s, s ^ bit) for s in range(tiles)])

    def spread(value):
        return lax.all_to_all(value, "tile", split_axis=0, concat_axis=0, tiled=True)

    wide = ufac.shape[2]
    step = rows * 2 * lanes // wide
    assert wide % (2 * lanes) == 0 and step % 16 == 0
    to_far, to_near, own = call(
        prepare_kernel,
        (
            shape((2 * rows + 2 * step, wide), bf16),
            shape((2 * rows + step, wide), bf16),
            shape((rows, lanes), f32),
        ),
        data, ufac, **static,
    )
    far = exchange(to_far, 2)
    near = exchange(to_near, 1)
    far_near = exchange(far, 1)

    chunks = shape((tiles, rank, lanes), bf16)
    coeffs = call(first_kernel, chunks, x_init, vfac, **static)
    estimate = x_init
    for iteration in range(ITERS):
        last = iteration == ITERS - 1
        outs = (chunks, shape((group, rows, lanes), f32)) if last else (chunks,)
        row = call(row_kernel, outs, spread(coeffs), own, ufac, near, far, far_near, width=width)
        if last:
            misfit = row[1]
            misfit_far = exchange(misfit[2:], 2)
            misfit_near = exchange(misfit[1], 1)
            misfit_far_near = exchange(misfit_far, 1)
        adjoint = spread(row[0])
        if last:
            estimate = call(last_kernel, shape(x_init.shape, f32), adjoint, estimate, vfac, **static)
        else:
            estimate, coeffs = call(
                middle_kernel, (shape(x_init.shape, f32), chunks), adjoint, estimate, vfac, **static
            )
    residual = call(
        residual_kernel, shape(data.shape, f32), misfit, misfit_near, misfit_far, misfit_far_near, **static
    )
    return (estimate, residual)


def solution(mesh):
    in_specs = (
        P("freq", "tile", None),
        P("freq", "tile", None),
        P("freq", "tile", None),
        P("freq", None, None, "tile"),
    )
    out_specs = (P("freq", "tile", None), P("freq", "tile", None))
    return jax.shard_map(body, mesh=mesh, in_specs=in_specs, out_specs=out_specs, check_vma=False)
```

time: 85.9 us -> 77.8 us (0.906)
  waiting for transfers between devices: 37.1 us -> 12 us
  blocking collectives: 13.9 us -> 35.2 us
  Pallas kernels: 0 us -> 17.1 us
  starting transfers between devices: 14.8 us -> 7.63 us
  matrix products: 7.03 us -> 0 us
  other arithmetic: 6.81 us -> 0 us
    all_to_all x3 -> x1, waiting for transfers between devices: 37.1 us -> 4.14 us  [spread(): lax.all_to_all(value, 'tile', split_axis=0, concat_axis=0, tiled=True)]
    all_to_all x1 -> x3, blocking collectives: 13.9 us -> 35.2 us  [spread(): lax.all_to_all(value, 'tile', split_axis=0, concat_axis=0, tiled=True)]
    pallas_call x0 -> x7, Pallas kernels: none -> 17.1 us  [call(): pl.pallas_call(functools.partial(kernel, **static), out_shape=out_shape,...]
    all_to_all x3 -> x1, starting transfers between devices: 14.8 us -> 3.49 us  [spread(): lax.all_to_all(value, 'tile', split_axis=0, concat_axis=0, tiled=True)]
    ppermute x0 -> x6, waiting for transfers between devices: none -> 7.89 us  [exchange(): return lax.ppermute(value, 'tile', [(s, s ^ bit) for s in range(tiles)])]
    dot_general x32 -> x0, matrix products: 7.03 us -> none  [single(): jnp.einsum(pattern, factor_part, vector_part, preferred_element_type=jnp....]
    ppermute x0 -> x6, starting transfers between devices: none -> 4.14 us  [exchange(): return lax.ppermute(value, 'tile', [(s, s ^ bit) for s in range(tiles)])]
    convert_element_type x4 -> x0, other arithmetic: 2.41 us -> none  [the longest x2 1.64 us: body(): xlow = estimate.astype(jnp.bfloat16)]
  transfers between devices with their start and end apart: 3 -> 7, of which waited for: 3 -> 3; matrix products, arithmetic and copies ran while one was open for 2% -> 1% of each run, Pallas kernels for 0% -> 6%
where the time goes in v1:
time: 77.8 us; the launch traced here: 77.1 us
  blocking collectives  35.2 us (45%)
  Pallas kernels  17.1 us (22%)
  waiting for transfers between devices  12 us (15%)
  starting transfers between devices  7.63 us (10%)
  local copies, waits for them, and re-layouts  4.45 us (6%)
    all_to_all x3, blocking collectives, spread(): lax.all_to_all(value, 'tile', split_axis=0, concat_axis=0, tiled=True)  35.2 us
    pallas_call x7, Pallas kernels, call(): pl.pallas_call(functools.partial(kernel, **static), out_shape=out_shape,...  17.1 us
    ppermute x6, waiting for transfers between devices, exchange(): return lax.ppermute(value, 'tile', [(s, s ^ bit) for s in range(tiles)])  7.89 us
    ppermute x6, starting transfers between devices, exchange(): return lax.ppermute(value, 'tile', [(s, s ^ bit) for s in range(tiles)])  4.14 us
    all_to_all x1, waiting for transfers between devices, spread(): lax.all_to_all(value, 'tile', split_axis=0, concat_axis=0, tiled=True)  4.14 us
    all_to_all x1, starting transfers between devices, spread(): lax.all_to_all(value, 'tile', split_axis=0, concat_axis=0, tiled=True)  3.49 us
    unnamed x14, local copies, waits for them, and re-layouts  2.65 us
  transfers between devices with their start and end apart: 7, of which 3 were waited for; matrix products, arithmetic and copies ran while one was open for 1% of the time, Pallas kernels for 6%

profile of v1, /device:TPU:0, one launch (start us, length us, event | category | flops | bytes accessed | tf_op | source)
XLA Modules:
  0.0 77.1 jit_solution(7267528329605629397)
XLA Ops:
  0.6 2.0 %prepare_kernel.1 = (bf16[512,256]{1,0:T(8,128)(2,1)}, bf16[384,256]{1,0:T(8,128)(2,1)}, f32[128,128]{1,0:T(8,128)}) custom-call(f32[2,128,256]{2,1,0:T(8,128)} %data.1, bf16[2,128,256]{2,1,0:T(8,128)(2,1)} %ufac.5), custom_call_target="tpu_custom_call" | custom-call | tf_op jit(solution)/shard_map/prepare_kernel/pallas_call | solution.py:203
  2.6 3.0 %collective-permute-start.1 = (bf16[512,256]{1,0:T(8,128)(2,1)}, bf16[512,256]{1,0:T(8,128)(2,1)S(1)}, u32[]{:S(2)}, u32[]{:S(2)}) collective-permute-start(bf16[512,256]{1,0:T(8,128)(2,1)} %get-tuple-element.11), channel_id=1, source_target_pairs={{0,2},{1,3},{2,0},{3,1},{4,6},{5,7},{6,4},{7,5},{8,10},{9,11},{10,... | collective-permute-start | bytes 786440 | tf_op jit(solution)/shard_map/ppermute | solution.py:223
  5.6 6.5 %collective-permute-done.1.far = bf16[512,256]{1,0:T(8,128)(2,1)S(1)} collective-permute-done((bf16[512,256]{1,0:T(8,128)(2,1)}, bf16[512,256]{1,0:T(8,128)(2,1)S(1)}, u32[]{:S(2)}, u32[]{:S(2)}) %collective-permute-start.1) | collective-permute-done | bytes 262176 | tf_op jit(solution)/shard_map/ppermute | solution.py:223
  12.1 0.0 collective-permute-start.2
  12.1 0.5 collective-permute-start
  12.6 2.2 %first_kernel.1 = bf16[16,16,128]{2,1,0:T(8,128)(2,1)} custom-call(f32[2,512,256]{2,1,0:T(8,128)} %x.3, bf16[2,4,16,512]{3,2,1,0:T(8,128)(2,1)} %vfac.5), custom_call_target="tpu_custom_call" | custom-call | tf_op jit(solution)/shard_map/first_kernel/pallas_call | solution.py:203
  14.8 13.2 %all_to_all.20.coeffs = bf16[16,16,128]{2,1,0:T(8,128)(2,1)} all-to-all(bf16[16,16,128]{2,1,0:T(8,128)(2,1)} %first_kernel.1), channel_id=1, replica_groups=mesh['freq'=2,'tile'=16] {'tile'}, dimensions={0} | all-to-all | bytes 131072 | tf_op jit(solution)/shard_map/all_to_all | solution.py:226
  27.9 0.0 collective-permute-done.near
  28.0 0.0 collective-permute-done.2.far_near
  28.0 0.0 copy-start.1
  28.0 0.7 copy-done.2
  28.6 0.1 copy-done.1
  28.7 2.7 %row_kernel.2 = bf16[16,16,128]{2,1,0:T(8,128)(2,1)} custom-call(bf16[16,16,128]{2,1,0:T(8,128)(2,1)} %all_to_all.20.coeffs, f32[128,128]{1,0:T(8,128)} %get-tuple-element.9.own, bf16[2,128,256]{2,1,0:T(8,128)(2,1)} %ufac.5, bf16[384,256]{1,0:T(8,128)(2,1)} %copy-done.2, bf16[512,256]{1,0:T(8,128)(2,1)} %copy-done, bf16[512,256]{1,0:T(8,128)(2,1)} %copy-done.1), custom_call_target="tpu_custom_call" | custom-call | tf_op jit(solution)/shard_map/row_kernel/pallas_call | solution.py:203
  31.4 11.0 %all_to_all.21.adjoint = bf16[16,16,128]{2,1,0:T(8,128)(2,1)} all-to-all(bf16[16,16,128]{2,1,0:T(8,128)(2,1)} %row_kernel.2), channel_id=1, replica_groups=mesh['freq'=2,'tile'=16] {'tile'}, dimensions={0} | all-to-all | bytes 131072 | tf_op jit(solution)/shard_map/all_to_all | solution.py:226
  42.4 2.9 %middle_kernel.1 = (f32[2,512,256]{2,1,0:T(8,128)}, bf16[16,16,128]{2,1,0:T(8,128)(2,1)}) custom-call(bf16[16,16,128]{2,1,0:T(8,128)(2,1)} %all_to_all.21.adjoint, f32[2,512,256]{2,1,0:T(8,128)} %x.3, bf16[2,4,16,512]{3,2,1,0:T(8,128)(2,1)} %vfac.5), custom_call_target="tpu_custom_call" | custom-call | tf_op jit(solution)/shard_map/middle_kernel/pallas_call | solution.py:203
  45.3 11.0 %all_to_all.22.coeffs = bf16[16,16,128]{2,1,0:T(8,128)(2,1)} all-to-all(bf16[16,16,128]{2,1,0:T(8,128)(2,1)} %get-tuple-element.12), channel_id=1, replica_groups=mesh['freq'=2,'tile'=16] {'tile'}, dimensions={0} | all-to-all | bytes 131072 | tf_op jit(solution)/shard_map/all_to_all | solution.py:226
  56.3 2.7 %row_kernel.3 = (bf16[16,16,128]{2,1,0:T(8,128)(2,1)}, f32[4,128,128]{2,1,0:T(8,128)}) custom-call(bf16[16,16,128]{2,1,0:T(8,128)(2,1)} %all_to_all.22.coeffs, f32[128,128]{1,0:T(8,128)} %get-tuple-element.9.own, bf16[2,128,256]{2,1,0:T(8,128)(2,1)} %ufac.5, bf16[384,256]{1,0:T(8,128)(2,1)} %copy-done.2, bf16[512,256]{1,0:T(8,128)(2,1)} %copy-done, ...), custom_call_target="tpu_custom_call" | custom-call | tf_op jit(solution)/shard_map/row_kernel/pallas_call | solution.py:203
  59.0 0.9 %slice.7 = f32[2,128,128]{2,1,0:T(8,128)S(1)} slice(f32[4,128,128]{2,1,0:T(8,128)} %get-tuple-element.15.misfit), slice={[2:4], [0:128], [0:128]} | slice | bytes 262144 | tf_op jit(solution)/shard_map/slice | solution.py:253
  59.9 0.2 collective-permute-start.4
  60.1 3.5 %all-to-all-start.3 = ((bf16[16,16,128]{2,1,0:T(8,128)(2,1)}), bf16[16,16,128]{2,1,0:T(8,128)(2,1)S(1)}, u32[]{:S(2)}, u32[]{:S(2)}) async-start(bf16[16,16,128]{2,1,0:T(8,128)(2,1)} %get-tuple-element.13), calls=%async_computation.3 | async-start | bytes 131072 | tf_op jit(solution)/shard_map/all_to_all | solution.py:226
  63.6 1.4 %collective-permute-done.4.far = f32[2,128,128]{2,1,0:T(8,128)S(1)} collective-permute-done((f32[2,128,128]{2,1,0:T(8,128)S(1)}, f32[2,128,128]{2,1,0:T(8,128)S(1)}, u32[]{:S(2)}, u32[]{:S(2)}) %collective-permute-start.4) | collective-permute-done | bytes 131104 | tf_op jit(solution)/shard_map/ppermute | solution.py:223
  65.0 0.0 collective-permute-start.5
  65.0 0.9 %slice_bitcast_fusion = f32[128,128]{1,0:T(8,128)S(1)} fusion(f32[4,128,128]{2,1,0:T(8,128)} %get-tuple-element.15.misfit), kind=kLoop, calls=%fused_computation | loop fusion | bytes 131072 | tf_op jit(solution)/shard_map/squeeze | solution.py:254
  65.9 0.5 collective-permute-start.3
  66.3 4.1 %all-to-all-done.3.adjoint = bf16[16,16,128]{2,1,0:T(8,128)(2,1)S(1)} async-done(((bf16[16,16,128]{2,1,0:T(8,128)(2,1)}), bf16[16,16,128]{2,1,0:T(8,128)(2,1)S(1)}, u32[]{:S(2)}, u32[]{:S(2)}) %all-to-all-start.3) | async-done | bytes 65568 | tf_op jit(solution)/shard_map/all_to_all | solution.py:226
  70.5 0.6 copy-done.3
  71.1 2.8 %last_kernel.1 = f32[2,512,256]{2,1,0:T(8,128)} custom-call(bf16[16,16,128]{2,1,0:T(8,128)(2,1)} %copy-done.3, f32[2,512,256]{2,1,0:T(8,128)} %get-tuple-element.14.x, bf16[2,4,16,512]{3,2,1,0:T(8,128)(2,1)} %vfac.5), custom_call_target="tpu_custom_call" | custom-call | tf_op jit(solution)/shard_map/last_kernel/pallas_call | solution.py:203
  73.9 0.0 collective-permute-done.3.near
  73.9 0.0 collective-permute-done.5.far_near
  73.9 0.6 copy-done.6
  74.5 0.7 copy-done.5
  75.2 1.9 %residual_kernel.1 = f32[2,128,256]{2,1,0:T(8,128)} custom-call(f32[4,128,128]{2,1,0:T(8,128)} %get-tuple-element.15.misfit, f32[128,128]{1,0:T(8,128)} %copy-done.6, f32[2,128,128]{2,1,0:T(8,128)} %copy-done.4, f32[2,128,128]{2,1,0:T(8,128)} %copy-done.5), custom_call_target="tpu_custom_call" | custom-call | tf_op jit(solution)/shard_map/residual_kernel/pallas_call | solution.py:203
  (8 shorter events, 0.0 us)
Async XLA Ops:
  2.6 9.5 %collective-permute-start.1 = (bf16[512,256]{1,0:T(8,128)(2,1)}, bf16[512,256]{1,0:T(8,128)(2,1)S(1)}, u32[]{:S(2)}, u32[]{:S(2)}) collective-permute-start(bf16[512,256]{1,0:T(8,128)(2,1)} %get-tuple-element.11), channel_id=1, source_target_pairs={{0,2},{1,3},{2,0},{3,1},{4,6},{5,7},{6,4},{7,5},{8,10},{9,11},{10,... | collective-permute-start | bytes 786440 | tf_op jit(solution)/shard_map/ppermute | solution.py:223
  12.1 2.7 %copy-start = (bf16[512,256]{1,0:T(8,128)(2,1)}, bf16[512,256]{1,0:T(8,128)(2,1)S(1)}, u32[]{:S(2)}) copy-start(bf16[512,256]{1,0:T(8,128)(2,1)S(1)} %collective-permute-done.1.far) | copy-start | bytes 786436
  12.1 15.8 %collective-permute-start.2 = (bf16[512,256]{1,0:T(8,128)(2,1)S(1)}, bf16[512,256]{1,0:T(8,128)(2,1)S(1)}, u32[]{:S(2)}, u32[]{:S(2)}) collective-permute-start(bf16[512,256]{1,0:T(8,128)(2,1)S(1)} %collective-permute-done.1.far), channel_id=1, source_target_pairs={{0,1},{1,0},{2,3},{3,2},{4,5},{5,4},{6,7},{7,6},{8,9},{9,8},{10,11... | collective-permute-start | bytes 786440 | tf_op jit(solution)/shard_map/ppermute | solution.py:223
  12.1 15.8 %collective-permute-start = (bf16[384,256]{1,0:T(8,128)(2,1)}, bf16[384,256]{1,0:T(8,128)(2,1)S(1)}, u32[]{:S(2)}, u32[]{:S(2)}) collective-permute-start(bf16[384,256]{1,0:T(8,128)(2,1)} %get-tuple-element.10), channel_id=1, source_target_pairs={{0,1},{1,0},{2,3},{3,2},{4,5},{5,4},{6,7},{7,6},{8,9},{9,8},{10,11... | collective-permute-start | bytes 589832 | tf_op jit(solution)/shard_map/ppermute | solution.py:223
  27.9 0.7 copy-start.2
  28.0 0.8 copy-start.1
  59.9 5.0 %collective-permute-start.4 = (f32[2,128,128]{2,1,0:T(8,128)S(1)}, f32[2,128,128]{2,1,0:T(8,128)S(1)}, u32[]{:S(2)}, u32[]{:S(2)}) collective-permute-start(f32[2,128,128]{2,1,0:T(8,128)S(1)} %slice.7), channel_id=1, source_target_pairs={{0,2},{1,3},{2,0},{3,1},{4,6},{5,7},{6,4},{7,5},{8,10},{9,11},{10,... | collective-permute-start | bytes 393224 | tf_op jit(solution)/shard_map/ppermute | solution.py:223
  60.1 10.4 %all-to-all-start.3 = ((bf16[16,16,128]{2,1,0:T(8,128)(2,1)}), bf16[16,16,128]{2,1,0:T(8,128)(2,1)S(1)}, u32[]{:S(2)}, u32[]{:S(2)}) async-start(bf16[16,16,128]{2,1,0:T(8,128)(2,1)} %get-tuple-element.13), calls=%async_computation.3 | async-start | bytes 131072 | tf_op jit(solution)/shard_map/all_to_all | solution.py:226
  65.0 8.9 %copy-start.4 = (f32[2,128,128]{2,1,0:T(8,128)}, f32[2,128,128]{2,1,0:T(8,128)S(1)}, u32[]{:S(2)}) copy-start(f32[2,128,128]{2,1,0:T(8,128)S(1)} %collective-permute-done.4.far) | copy-start | bytes 393220
  65.0 8.9 %collective-permute-start.5 = (f32[2,128,128]{2,1,0:T(8,128)S(1)}, f32[2,128,128]{2,1,0:T(8,128)S(1)}, u32[]{:S(2)}, u32[]{:S(2)}) collective-permute-start(f32[2,128,128]{2,1,0:T(8,128)S(1)} %collective-permute-done.4.far), channel_id=1, source_target_pairs={{0,1},{1,0},{2,3},{3,2},{4,5},{5,4},{6,7},{7,6},{8,9},{9,8},{10,11... | collective-permute-start | bytes 393224 | tf_op jit(solution)/shard_map/ppermute | solution.py:223
  65.9 8.0 %collective-permute-start.3 = (f32[128,128]{1,0:T(8,128)S(1)}, f32[128,128]{1,0:T(8,128)S(1)}, u32[]{:S(2)}, u32[]{:S(2)}) collective-permute-start(f32[128,128]{1,0:T(8,128)S(1)} %slice_bitcast_fusion), channel_id=1, source_target_pairs={{0,1},{1,0},{2,3},{3,2},{4,5},{5,4},{6,7},{7,6},{8,9},{9,8},{10,11... | collective-permute-start | bytes 196616 | tf_op jit(solution)/shard_map/ppermute | solution.py:223
  70.5 0.6 copy-start.3
  73.9 0.6 copy-start.6
  74.5 0.7 copy-start.5

commit v2 on v1

--- a/solution.py
+++ b/solution.py
@@ -10,6 +10,7 @@
 ITERS = 2
 STEP = 0.4
 THRESHOLD = 0.4
+VMEM_LIMIT = 24 << 20
 
 f32 = jnp.float32
 bf16 = jnp.bfloat16
@@ -132,7 +133,10 @@
     for b, (wave, (ur, ui)) in enumerate(blocks):
         misfit = wave - (dot(ur, c) + dot(ui, ci))
         if maybe_misfit:
-            maybe_misfit[0][b] = misfit
+            if b < 2:
+                maybe_misfit[b][...] = misfit
+            else:
+                maybe_misfit[2][b - 2] = misfit
         mt = misfit.T.astype(bf16)
         mr, mi = mt[:width], mt[width:]
         turned = jnp.concatenate([mi, -mr], axis=0)
@@ -177,34 +181,60 @@
 
 
 def last_kernel(adjoint, x, vfac, x_new, *, group, width):
-    xr, xi = updated(adjoint, x, flat_factors(vfac), group=group, width=width)
-    x_new[0] = xr
-    x_new[1] = xi
+    def run(stage, sems):
+        parts = updated(adjoint, x, flat_factors(vfac), group=group, width=width)
+        copies = []
+        for k, part in enumerate(parts):
+            stage[k] = part
+            copies.append(pltpu.make_async_copy(stage.at[k], x_new.at[k], sems.at[k]))
+            copies[-1].start()
+        for copy in copies:
+            copy.wait()
+
+    pl.run_scoped(run, pltpu.VMEM(x.shape, f32), pltpu.SemaphoreType.DMA((2,)))
 
 
 def residual_kernel(misfit, near, far, far_near, out, *, group, width):
     q = group_index(group)
 
-    def place(scratch):
-        scratch[0] = misfit[0]
+    def place(scratch, stage, sem):
+        scratch[0] = misfit[...]
         scratch[1] = near[...]
         scratch[2] = far[0]
         scratch[3] = far_near[1]
         pieces = [scratch[jnp.bitwise_xor(q, s)] for s in range(group)]
         for k in range(group // 2):
             re, im = interleave(pieces[2 * k], pieces[2 * k + 1])
-            out[0, :, 2 * width * k:2 * width * (k + 1)] = re
-            out[1, :, 2 * width * k:2 * width * (k + 1)] = im
-
-    pl.run_scoped(place, pltpu.VMEM(misfit.shape, f32))
+            stage[0, :, 2 * width * k:2 * width * (k + 1)] = re
+            stage[1, :, 2 * width * k:2 * width * (k + 1)] = im
+        copy = pltpu.make_async_copy(stage, out, sem)
+        copy.start()
+        copy.wait()
+
+    pl.run_scoped(
+        place,
+        pltpu.VMEM((group,) + misfit.shape, f32),
+        pltpu.VMEM(out.shape, f32),
+        pltpu.SemaphoreType.DMA(()),
+    )
 
 
 def call(kernel, out_shape, *args, **static):
+    on_chip = pl.BlockSpec(memory_space=pltpu.VMEM)
+    off_chip = pl.BlockSpec(memory_space=pl.ANY)
+    many = isinstance(out_shape, tuple)
+
+    def spec(out):
+        return off_chip if isinstance(out, jax.ShapeDtypeStruct) else on_chip
+
     return pl.pallas_call(
         functools.partial(kernel, **static),
         out_shape=out_shape,
+        in_specs=[on_chip] * len(args),
+        out_specs=tuple(map(spec, out_shape)) if many else spec(out_shape),
+        compiler_params=pltpu.CompilerParams(vmem_limit_bytes=VMEM_LIMIT),
         name=kernel.__name__,
-    )(*args)
+    )(*(pltpu.with_memory_space_constraint(arg, pltpu.VMEM) for arg in args))
 
 
 def body(data, x_init, ufac, vfac):
@@ -217,7 +247,8 @@
     width = points // group
     lanes = 2 * width
     static = dict(group=group, width=width)
-    shape = jax.ShapeDtypeStruct
+    shape = pltpu.VMEM
+    result = jax.ShapeDtypeStruct
 
     def exchange(value, bit):
         return lax.ppermute(value, "tile", [(s, s ^ bit) for s in range(tiles)])
@@ -239,29 +270,29 @@
     )
     far = exchange(to_far, 2)
     near = exchange(to_near, 1)
-    far_near = exchange(far, 1)
-
     chunks = shape((tiles, rank, lanes), bf16)
     coeffs = call(first_kernel, chunks, x_init, vfac, **static)
+    far_near = exchange(lax.optimization_barrier((far, coeffs))[0], 1)
     estimate = x_init
     for iteration in range(ITERS):
         last = iteration == ITERS - 1
-        outs = (chunks, shape((group, rows, lanes), f32)) if last else (chunks,)
+        block = shape((rows, lanes), f32)
+        outs = (chunks, block, block, shape((2, rows, lanes), f32)) if last else (chunks,)
         row = call(row_kernel, outs, spread(coeffs), own, ufac, near, far, far_near, width=width)
         if last:
-            misfit = row[1]
-            misfit_far = exchange(misfit[2:], 2)
-            misfit_near = exchange(misfit[1], 1)
+            _, misfit, to_near, to_far = row
+            misfit_far = exchange(to_far, 2)
+            misfit_near = exchange(to_near, 1)
             misfit_far_near = exchange(misfit_far, 1)
         adjoint = spread(row[0])
         if last:
-            estimate = call(last_kernel, shape(x_init.shape, f32), adjoint, estimate, vfac, **static)
+            estimate = call(last_kernel, result(x_init.shape, f32), adjoint, estimate, vfac, **static)
         else:
             estimate, coeffs = call(
                 middle_kernel, (shape(x_init.shape, f32), chunks), adjoint, estimate, vfac, **static
             )
     residual = call(
-        residual_kernel, shape(data.shape, f32), misfit, misfit_near, misfit_far, misfit_far_near, **static
+        residual_kernel, result(data.shape, f32), misfit, misfit_near, misfit_far, misfit_far_near, **static
     )
     return (estimate, residual)
 

time: 77.8 us -> 65.7 us (0.84)
  Pallas kernels: 17.1 us -> 6.05 us
  waiting for transfers between devices: 12 us -> 16 us
  blocking collectives: 35.2 us -> 31.8 us
  local copies, waits for them, and re-layouts: 4.45 us -> 3.12 us
    pallas_call x7, Pallas kernels: 17.1 us -> 6.05 us  [call(): pl.pallas_call(functools.partial(kernel, **static), out_shape=out_shape,...]
    all_to_all x3, blocking collectives: 35.2 us -> 31.8 us  [spread(): lax.all_to_all(value, 'tile', split_axis=0, concat_axis=0, tiled=True)]
    all_to_all x1, waiting for transfers between devices: 4.14 us -> 6.39 us  [spread(): lax.all_to_all(value, 'tile', split_axis=0, concat_axis=0, tiled=True)]
    ppermute x6, waiting for transfers between devices: 7.89 us -> 9.62 us  [exchange(): return lax.ppermute(value, 'tile', [(s, s ^ bit) for s in range(tiles)])]
    slice x1 -> x0, local copies, waits for them, and re-layouts: 0.91 us -> none  [body(): misfit_far = exchange(misfit[2:], 2)]
    squeeze x1 -> x0, local copies, waits for them, and re-layouts: 0.89 us -> none  [body(): misfit_near = exchange(misfit[1], 1)]
    unnamed x14 -> x12, local copies, waits for them, and re-layouts: 2.65 us -> 3.12 us
  transfers between devices with their start and end apart: 7 -> 7, of which waited for: 3 -> 3; matrix products, arithmetic and copies ran while one was open for 1% -> 0% of each run, Pallas kernels for 6% -> 3%
where the time goes in v2:
time: 65.7 us; the launch traced here: 65.3 us
  blocking collectives  31.8 us (48%)
  waiting for transfers between devices  16 us (24%)
  starting transfers between devices  7.66 us (12%)
  Pallas kernels  6.05 us (9%)
  local copies, waits for them, and re-layouts  3.12 us (5%)
  between operations  0.71 us (1%)
    all_to_all x3, blocking collectives, spread(): lax.all_to_all(value, 'tile', split_axis=0, concat_axis=0, tiled=True)  31.8 us
    ppermute x6, waiting for transfers between devices, exchange(): return lax.ppermute(value, 'tile', [(s, s ^ bit) for s in range(tiles)])  9.62 us
    all_to_all x1, waiting for transfers between devices, spread(): lax.all_to_all(value, 'tile', split_axis=0, concat_axis=0, tiled=True)  6.39 us
    pallas_call x7, Pallas kernels, call(): pl.pallas_call(functools.partial(kernel, **static), out_shape=out_shape,...  6.05 us
    ppermute x6, starting transfers between devices, exchange(): return lax.ppermute(value, 'tile', [(s, s ^ bit) for s in range(tiles)])  4.15 us
    all_to_all x1, starting transfers between devices, spread(): lax.all_to_all(value, 'tile', split_axis=0, concat_axis=0, tiled=True)  3.5 us
    unnamed x12, local copies, waits for them, and re-layouts  3.12 us
  transfers between devices with their start and end apart: 7, of which 3 were waited for; matrix products, arithmetic and copies ran while one was open for 0% of the time, Pallas kernels for 3%

profile of v2, /device:TPU:0, one launch (start us, length us, event | category | flops | bytes accessed | tf_op | source)
XLA Modules:
  0.0 65.3 jit_solution(12279466582142686629)
XLA Ops:
  0.6 0.0 copy-start.2
  0.6 0.0 copy-start.3
  0.7 0.9 %copy-done.3 = bf16[2,128,256]{2,1,0:T(8,128)(2,1)S(1)} copy-done((bf16[2,128,256]{2,1,0:T(8,128)(2,1)S(1)}, bf16[2,128,256]{2,1,0:T(8,128)(2,1)}, u32[]{:S(2)}) %copy-start.3) | copy-done | bytes 131096
  1.6 0.9 %copy-done.5 = f32[2,128,256]{2,1,0:T(8,128)S(1)} copy-done((f32[2,128,256]{2,1,0:T(8,128)S(1)}, f32[2,128,256]{2,1,0:T(8,128)}, u32[]{:S(2)}) %copy-start.5) | copy-done | bytes 262168
  2.5 0.2 prepare_kernel.1
  2.7 3.1 %collective-permute-start.1 = (bf16[512,256]{1,0:T(8,128)(2,1)S(1)}, bf16[512,256]{1,0:T(8,128)(2,1)S(1)}, u32[]{:S(2)}, u32[]{:S(2)}) collective-permute-start(bf16[512,256]{1,0:T(8,128)(2,1)S(1)} %get-tuple-element.14), channel_id=1, source_target_pairs={{0,2},{1,3},{2,0},{3,1},{4,6},{5,7},{6,4},{7,5},{8,10},{9,11},{10,... | collective-permute-start | bytes 786440 | tf_op jit(solution)/shard_map/ppermute | solution.py:254
  5.8 1.2 %copy-done = f32[2,512,256]{2,1,0:T(8,128)S(1)} copy-done((f32[2,512,256]{2,1,0:T(8,128)S(1)}, f32[2,512,256]{2,1,0:T(8,128)}, u32[]{:S(2)}) %copy-start) | copy-done | bytes 1048600
  7.0 0.3 first_kernel.1
  7.4 0.0 copy-start.4
  7.4 4.7 %collective-permute-done.1.far = bf16[512,256]{1,0:T(8,128)(2,1)S(1)} collective-permute-done((bf16[512,256]{1,0:T(8,128)(2,1)S(1)}, bf16[512,256]{1,0:T(8,128)(2,1)S(1)}, u32[]{:S(2)}, u32[]{:S(2)}) %collective-permute-start.1) | collective-permute-done | bytes 262176 | tf_op jit(solution)/shard_map/ppermute | solution.py:254
  12.1 0.0 collective-permute-start.2
  12.1 0.5 collective-permute-start
  12.6 12.8 %all_to_all.20.coeffs = bf16[16,16,128]{2,1,0:T(8,128)(2,1)S(1)} all-to-all(bf16[16,16,128]{2,1,0:T(8,128)(2,1)S(1)} %first_kernel.1), channel_id=1, replica_groups=mesh['freq'=2,'tile'=16] {'tile'}, dimensions={0} | all-to-all | bytes 131072 | tf_op jit(solution)/shard_map/all_to_all | solution.py:257
  25.5 0.0 collective-permute-done.near
  25.5 0.0 collective-permute-done.2.far_near
  25.5 0.0 copy-done.4
  25.5 0.8 %row_kernel.2 = bf16[16,16,128]{2,1,0:T(8,128)(2,1)S(1)} custom-call(bf16[16,16,128]{2,1,0:T(8,128)(2,1)S(1)} %all_to_all.20.coeffs, f32[128,128]{1,0:T(8,128)S(1)} %get-tuple-element.12.own, bf16[2,128,256]{2,1,0:T(8,128)(2,1)S(1)} %copy-done.4, bf16[384,256]{1,0:T(8,128)(2,1)S(1)} %collective-permute-done.near, ...), custom_call_target="tpu_custom_call" | custom-call | tf_op jit(solution)/shard_map/row_kernel/pallas_call | solution.py:230
  26.3 9.5 %all_to_all.21.adjoint = bf16[16,16,128]{2,1,0:T(8,128)(2,1)S(1)} all-to-all(bf16[16,16,128]{2,1,0:T(8,128)(2,1)S(1)} %row_kernel.2), channel_id=1, replica_groups=mesh['freq'=2,'tile'=16] {'tile'}, dimensions={0} | all-to-all | bytes 131072 | tf_op jit(solution)/shard_map/all_to_all | solution.py:257
  35.7 0.0 copy-done.1
  35.8 0.9 %middle_kernel.1 = (f32[2,512,256]{2,1,0:T(8,128)S(1)}, bf16[16,16,128]{2,1,0:T(8,128)(2,1)S(1)}) custom-call(bf16[16,16,128]{2,1,0:T(8,128)(2,1)S(1)} %all_to_all.21.adjoint, f32[2,512,256]{2,1,0:T(8,128)S(1)} %copy-done.1, bf16[2,4,16,512]{3,2,1,0:T(8,128)(2,1)S(1)} %copy-done.2), custom_call_target="tpu_custom_call" | custom-call | tf_op jit(solution)/shard_map/middle_kernel/pallas_call | solution.py:230
  36.7 9.5 %all_to_all.22.coeffs = bf16[16,16,128]{2,1,0:T(8,128)(2,1)S(1)} all-to-all(bf16[16,16,128]{2,1,0:T(8,128)(2,1)S(1)} %get-tuple-element.16), channel_id=1, replica_groups=mesh['freq'=2,'tile'=16] {'tile'}, dimensions={0} | all-to-all | bytes 131072 | tf_op jit(solution)/shard_map/all_to_all | solution.py:257
  46.2 1.4 %row_kernel.3 = (bf16[16,16,128]{2,1,0:T(8,128)(2,1)}, f32[128,128]{1,0:T(8,128)S(1)}, f32[128,128]{1,0:T(8,128)S(1)}, f32[2,128,128]{2,1,0:T(8,128)S(1)}) custom-call(bf16[16,16,128]{2,1,0:T(8,128)(2,1)S(1)} %all_to_all.22.coeffs, f32[128,128]{1,0:T(8,128)S(1)} %get-tuple-element.12.own, bf16[2,128,256]{2,1,0:T(8,128)(2,1)S(1)} %copy-done.4, ...), custom_call_target="tpu_custom_call" | custom-call | tf_op jit(solution)/shard_map/row_kernel/pallas_call | solution.py:230
  47.6 0.1 collective-permute-start.4
  47.7 4.9 %collective-permute-done.4.far = f32[2,128,128]{2,1,0:T(8,128)S(1)} collective-permute-done((f32[2,128,128]{2,1,0:T(8,128)S(1)}, f32[2,128,128]{2,1,0:T(8,128)S(1)}, u32[]{:S(2)}, u32[]{:S(2)}) %collective-permute-start.4) | collective-permute-done | bytes 131104 | tf_op jit(solution)/shard_map/ppermute | solution.py:254
  52.5 0.0 collective-permute-start.5
  52.5 3.5 %all-to-all-start.3 = ((bf16[16,16,128]{2,1,0:T(8,128)(2,1)}), bf16[16,16,128]{2,1,0:T(8,128)(2,1)S(1)}, u32[]{:S(2)}, u32[]{:S(2)}) async-start(bf16[16,16,128]{2,1,0:T(8,128)(2,1)} %get-tuple-element.17), calls=%async_computation.3 | async-start | bytes 131072 | tf_op jit(solution)/shard_map/all_to_all | solution.py:257
  56.1 0.5 collective-permute-start.3
  56.5 6.4 %all-to-all-done.3.adjoint = bf16[16,16,128]{2,1,0:T(8,128)(2,1)S(1)} async-done(((bf16[16,16,128]{2,1,0:T(8,128)(2,1)}), bf16[16,16,128]{2,1,0:T(8,128)(2,1)S(1)}, u32[]{:S(2)}, u32[]{:S(2)}) %all-to-all-start.3) | async-done | bytes 65568 | tf_op jit(solution)/shard_map/all_to_all | solution.py:257
  62.9 1.6 %last_kernel.1 = f32[2,512,256]{2,1,0:T(8,128)} custom-call(bf16[16,16,128]{2,1,0:T(8,128)(2,1)S(1)} %all-to-all-done.3.adjoint, f32[2,512,256]{2,1,0:T(8,128)S(1)} %get-tuple-element.18.x, bf16[2,4,16,512]{3,2,1,0:T(8,128)(2,1)S(1)} %copy-done.2), custom_call_target="tpu_custom_call" | custom-call | tf_op jit(solution)/shard_map/last_kernel/pallas_call | solution.py:230
  64.5 0.0 collective-permute-done.3.near
  64.5 0.0 collective-permute-done.5.far_near
  64.5 0.9 %residual_kernel.1 = f32[2,128,256]{2,1,0:T(8,128)} custom-call(f32[128,128]{1,0:T(8,128)S(1)} %get-tuple-element.19.misfit, f32[128,128]{1,0:T(8,128)S(1)} %collective-permute-done.3.near, f32[2,128,128]{2,1,0:T(8,128)S(1)} %collective-permute-done.4.far, f32[2,128,128]{2,1,0:T(8,128)S(1)} %collective-permute-done.5.far_near), custom_call_target="tpu_custom_call" | custom-call | tf_op jit(solution)/shard_map/residual_kernel/pallas_call | solution.py:230
  (4 shorter events, 0.0 us)
Async XLA Ops:
  0.6 5.2 %copy-start.2 = (bf16[2,4,16,512]{3,2,1,0:T(8,128)(2,1)S(1)}, bf16[2,4,16,512]{3,2,1,0:T(8,128)(2,1)}, u32[]{:S(2)}) copy-start(bf16[2,4,16,512]{3,2,1,0:T(8,128)(2,1)} %vfac.5) | copy-start | bytes 393220
  0.6 0.9 %copy-start.3 = (bf16[2,128,256]{2,1,0:T(8,128)(2,1)S(1)}, bf16[2,128,256]{2,1,0:T(8,128)(2,1)}, u32[]{:S(2)}) copy-start(bf16[2,128,256]{2,1,0:T(8,128)(2,1)} %ufac.5) | copy-start | bytes 393220
  1.6 0.9 %copy-start.5 = (f32[2,128,256]{2,1,0:T(8,128)S(1)}, f32[2,128,256]{2,1,0:T(8,128)}, u32[]{:S(2)}) copy-start(f32[2,128,256]{2,1,0:T(8,128)} %data.1) | copy-start | bytes 786436
  2.7 9.4 %collective-permute-start.1 = (bf16[512,256]{1,0:T(8,128)(2,1)S(1)}, bf16[512,256]{1,0:T(8,128)(2,1)S(1)}, u32[]{:S(2)}, u32[]{:S(2)}) collective-permute-start(bf16[512,256]{1,0:T(8,128)(2,1)S(1)} %get-tuple-element.14), channel_id=1, source_target_pairs={{0,2},{1,3},{2,0},{3,1},{4,6},{5,7},{6,4},{7,5},{8,10},{9,11},{10,... | collective-permute-start | bytes 786440 | tf_op jit(solution)/shard_map/ppermute | solution.py:254
  5.8 1.2 %copy-start = (f32[2,512,256]{2,1,0:T(8,128)S(1)}, f32[2,512,256]{2,1,0:T(8,128)}, u32[]{:S(2)}) copy-start(f32[2,512,256]{2,1,0:T(8,128)} %x.3) | copy-start | bytes 3145732
  7.0 28.7 %copy-start.1 = (f32[2,512,256]{2,1,0:T(8,128)S(1)}, f32[2,512,256]{2,1,0:T(8,128)}, u32[]{:S(2)}) copy-start(f32[2,512,256]{2,1,0:T(8,128)} %x.3) | copy-start | bytes 3145732
  7.4 18.1 %copy-start.4 = (bf16[2,128,256]{2,1,0:T(8,128)(2,1)S(1)}, bf16[2,128,256]{2,1,0:T(8,128)(2,1)}, u32[]{:S(2)}) copy-start(bf16[2,128,256]{2,1,0:T(8,128)(2,1)} %ufac.5) | copy-start | bytes 393220
  12.1 13.4 %collective-permute-start.2 = (bf16[512,256]{1,0:T(8,128)(2,1)S(1)}, bf16[512,256]{1,0:T(8,128)(2,1)S(1)}, u32[]{:S(2)}, u32[]{:S(2)}) collective-permute-start(bf16[512,256]{1,0:T(8,128)(2,1)S(1)} %collective-permute-done.1.far), channel_id=1, source_target_pairs={{0,1},{1,0},{2,3},{3,2},{4,5},{5,4},{6,7},{7,6},{8,9},{9,8},{10,11... | collective-permute-start | bytes 786440 | tf_op jit(solution)/shard_map/ppermute | solution.py:254
  12.1 13.4 %collective-permute-start = (bf16[384,256]{1,0:T(8,128)(2,1)S(1)}, bf16[384,256]{1,0:T(8,128)(2,1)S(1)}, u32[]{:S(2)}, u32[]{:S(2)}) collective-permute-start(bf16[384,256]{1,0:T(8,128)(2,1)S(1)} %get-tuple-element.13), channel_id=1, source_target_pairs={{0,1},{1,0},{2,3},{3,2},{4,5},{5,4},{6,7},{7,6},{8,9},{9,8},{10,11... | collective-permute-start | bytes 589832 | tf_op jit(solution)/shard_map/ppermute | solution.py:254
  47.6 5.0 %collective-permute-start.4 = (f32[2,128,128]{2,1,0:T(8,128)S(1)}, f32[2,128,128]{2,1,0:T(8,128)S(1)}, u32[]{:S(2)}, u32[]{:S(2)}) collective-permute-start(f32[2,128,128]{2,1,0:T(8,128)S(1)} %get-tuple-element.21), channel_id=1, source_target_pairs={{0,2},{1,3},{2,0},{3,1},{4,6},{5,7},{6,4},{7,5},{8,10},{9,11},{10,... | collective-permute-start | bytes 393224 | tf_op jit(solution)/shard_map/ppermute | solution.py:254
  52.5 11.9 %collective-permute-start.5 = (f32[2,128,128]{2,1,0:T(8,128)S(1)}, f32[2,128,128]{2,1,0:T(8,128)S(1)}, u32[]{:S(2)}, u32[]{:S(2)}) collective-permute-start(f32[2,128,128]{2,1,0:T(8,128)S(1)} %collective-permute-done.4.far), channel_id=1, source_target_pairs={{0,1},{1,0},{2,3},{3,2},{4,5},{5,4},{6,7},{7,6},{8,9},{9,8},{10,11... | collective-permute-start | bytes 393224 | tf_op jit(solution)/shard_map/ppermute | solution.py:254
  52.5 10.4 %all-to-all-start.3 = ((bf16[16,16,128]{2,1,0:T(8,128)(2,1)}), bf16[16,16,128]{2,1,0:T(8,128)(2,1)S(1)}, u32[]{:S(2)}, u32[]{:S(2)}) async-start(bf16[16,16,128]{2,1,0:T(8,128)(2,1)} %get-tuple-element.17), calls=%async_computation.3 | async-start | bytes 131072 | tf_op jit(solution)/shard_map/all_to_all | solution.py:257
  56.1 8.4 %collective-permute-start.3 = (f32[128,128]{1,0:T(8,128)S(1)}, f32[128,128]{1,0:T(8,128)S(1)}, u32[]{:S(2)}, u32[]{:S(2)}) collective-permute-start(f32[128,128]{1,0:T(8,128)S(1)} %get-tuple-element.20), channel_id=1, source_target_pairs={{0,1},{1,0},{2,3},{3,2},{4,5},{5,4},{6,7},{7,6},{8,9},{9,8},{10,11... | collective-permute-start | bytes 196616 | tf_op jit(solution)/shard_map/ppermute | solution.py:254
